TPU v7x, 256 devices: a whole 4x4x8 slice. The times are simulated.
256 devices in a mesh: expert: 32 (over z, y), tensor: 4 (over x), dp: 2 (over core).
Axes of the slice: x: 4, y: 4, z: 8, core: 2. Of those that a mesh axis runs over, the one named last changes fastest.
Arguments:
- tokens: bfloat16 [1024, 7168], P(('expert', 'dp')), may hold values from -6 to 6
- expert_ids: int32 [1024, 8], P(('expert', 'dp')), may hold values from 0 to 31, all different within a row; in each aligned block of 16 rows (0 to 15, 16 to 31, ...) at most 8 rows name the same one
- route_scores: float32 [1024, 8], P(('expert', 'dp')), may hold values from 0.05 to 1
- gate_weight: bfloat16 [32, 7168, 2048], P('expert', 'dp', 'tensor'), may hold values from -0.0625 to 0.0625
- up_weight: bfloat16 [32, 7168, 2048], P('expert', 'dp', 'tensor'), may hold values from -0.0625 to 0.0625
- down_weight: bfloat16 [32, 2048, 7168], P('expert', 'tensor', 'dp'), may hold values from -0.125 to 0.125
Outputs:
- mixed: bfloat16 [1024, 2, 3584], P(('expert', 'dp'), None, 'tensor')
Inputs may be any that keep to these rules, and one draw needn't show every extreme that they name: `expert_ids`: each token names 8 different experts. In each aligned block of 16 tokens (the tokens of one device along expert and dp) no expert is named by more than 8 tokens, a bound that some block reaches.
All inputs are finite; a program needn't handle non-finite values.
Results may differ from a plain program's by a relative error of at most 0.02.
Values may be sent and summed in bfloat16 or wider, within the bound.
A program may use at most 64 MiB of HBM per device.

v0:
```python
import jax
import jax.numpy as jnp
from jax import lax
from jax.sharding import PartitionSpec as P

TOP = 8
EXPERTS = 32
CAP = 8


def route_over_experts(blocks):
    return lax.all_to_all(blocks, "expert", split_axis=2, concat_axis=2, tiled=True)


def block_tables(block_ids, expert_count):
    pair_ids = block_ids.reshape(-1)
    expert_hot = (pair_ids[:, None] == jnp.arange(EXPERTS, dtype=jnp.int32)[None, :]).astype(
        jnp.int32
    )
    earlier = jnp.cumsum(expert_hot, axis=0) - expert_hot
    slot_index = jnp.sum(earlier * expert_hot, axis=1).reshape(block_ids.shape)
    expert_onehot = (
        block_ids[:, :, None] == jnp.arange(EXPERTS, dtype=jnp.int32)[None, None, :]
    ).astype(jnp.float32)
    expert_onehot = expert_onehot.reshape(
        block_ids.shape[0], TOP, expert_count, EXPERTS // expert_count
    )
    slot_onehot = (
        slot_index[:, :, None] == jnp.arange(CAP, dtype=jnp.int32)[None, None, :]
    ).astype(jnp.float32)
    return (expert_onehot, slot_onehot)


def placing_table(block_ids, expert_count):
    expert_onehot, slot_onehot = block_tables(block_ids, expert_count)
    return jnp.einsum("tkgl,tkc->lgct", expert_onehot, slot_onehot).astype(jnp.bfloat16)


def mixing_table(block_ids, block_scores, expert_count):
    expert_onehot, slot_onehot = block_tables(block_ids, expert_count)
    weights = (2.5 * block_scores / jnp.sum(block_scores, axis=1, keepdims=True)).astype(
        jnp.bfloat16
    )
    return jnp.einsum(
        "tk,tkgl,tkc->tglc", weights.astype(jnp.float32), expert_onehot, slot_onehot
    ).astype(jnp.bfloat16)


def on_device(tokens, expert_ids, route_scores, gate_weight, up_weight, down_weight):
    expert_count = lax.axis_size("expert")
    dp_count = lax.axis_size("dp")
    local_experts = gate_weight.shape[0]
    block_tokens = expert_ids.shape[0]
    placing = placing_table(expert_ids, expert_count)
    split_rows = tokens.reshape(block_tokens, dp_count, tokens.shape[1] // dp_count)
    outgoing = jnp.einsum(
        "lgct,tpd->lpgcd", placing, split_rows, preferred_element_type=jnp.float32
    ).astype(jnp.bfloat16)
    halves = lax.all_to_all(outgoing, "dp", split_axis=1, concat_axis=1, tiled=True)
    half_width = halves.shape[4]
    arrived = route_over_experts(halves)
    arrived = arrived.reshape(local_experts, dp_count * expert_count * CAP, half_width)
    gate = jnp.einsum("lrh,lhf->lrf", arrived, gate_weight, preferred_element_type=jnp.float32)
    up = jnp.einsum("lrh,lhf->lrf", arrived, up_weight, preferred_element_type=jnp.float32)
    gate, up = (
        lax.psum(gate.astype(jnp.bfloat16), "dp").astype(jnp.float32),
        lax.psum(up.astype(jnp.bfloat16), "dp").astype(jnp.float32),
    )
    hidden = (jax.nn.silu(gate) * up).astype(jnp.bfloat16)
    partial_value = jnp.einsum(
        "lrf,lfh->lrh", hidden, down_weight, preferred_element_type=jnp.float32
    )
    summed = lax.psum_scatter(
        partial_value.astype(jnp.bfloat16), "tensor", scatter_dimension=2, tiled=True
    ).astype(jnp.float32)
    summed = summed.astype(jnp.bfloat16).reshape(
        local_experts, dp_count, expert_count, CAP, summed.shape[2]
    )
    returned = route_over_experts(summed)
    results = lax.all_to_all(returned, "dp", split_axis=1, concat_axis=1, tiled=True)
    mixing = mixing_table(expert_ids, route_scores, expert_count)
    mixed = jnp.einsum("tglc,lhgcd->thd", mixing, results, preferred_element_type=jnp.float32)
    return mixed.astype(jnp.bfloat16)


def solution(mesh):
    in_specs = (
        P(("expert", "dp"), None),
        P(("expert", "dp"), None),
        P(("expert", "dp"), None),
        P("expert", "dp", "tensor"),
        P("expert", "dp", "tensor"),
        P("expert", "tensor", "dp"),
    )
    out_specs = P(("expert", "dp"), None, "tensor")
    return jax.shard_map(
        on_device, mesh=mesh, in_specs=in_specs, out_specs=out_specs, check_vma=False
    )
```

profile of v0, /device:TPU:1, one launch (start us, length us, event | category | flops | bytes accessed | tf_op | source)
XLA Modules:
  0.0 278.3 jit_solution(17216406574727778507)
XLA Ops:
  6.5 0.8 copy.22
  7.9 0.2 fusion.20
  8.3 2.0 fusion
  10.3 0.3 copy.27
  10.6 9.6 %all_to_all.20 = bf16[1,2,32,8,3584]{4,3,2,0,1:T(8,128)(2,1)S(1)} all-to-all(bf16[1,2,32,8,3584]{4,3,2,0,1:T(8,128)(2,1)S(1)} %copy.27), channel_id=1, replica_groups=mesh['expert'=32,'tensor'=4,'dp'=2] {'dp'}, dimensions={1} | all-to-all | bytes 7340032 | tf_op jit(solution)/shard_map/all_to_all | solution.py:59
  20.1 0.5 copy.28
  20.6 93.1 %all_to_all.21 = bf16[1,2,32,8,3584]{4,3,1,0,2:T(8,128)(2,1)S(1)} all-to-all(bf16[1,2,32,8,3584]{4,3,1,0,2:T(8,128)(2,1)S(1)} %copy.28), channel_id=1, replica_groups=mesh['expert'=32,'tensor'=4,'dp'=2] {'expert'}, dimensions={2} | all-to-all | bytes 7340032 | tf_op jit(solution)/shard_map/all_to_all | solution.py:12
  113.7 0.3 copy.29
  114.0 1.8 copy-done.1
  115.8 2.9 %fusion.13 = bf16[1,512,512]{2,1,0:T(8,128)(2,1)} fusion(bf16[512,3584]{1,0:T(8,128)(2,1)S(1)} %bitcast.71, bf16[1,3584,512]{2,1,0:T(8,128)(2,1)S(1)} %copy-done.1), kind=kOutput, calls=%fused_computation.15 | convolution fusion | flops 1879310336 | bytes 7864320 | tf_op jit(solution)/shard_map/lrh,lhf->lrf/dot_general | solution.py:64
  118.6 2.9 %fusion.16 = bf16[1,512,512]{2,1,0:T(8,128)(2,1)} fusion(bf16[512,3584]{1,0:T(8,128)(2,1)S(1)} %bitcast.72, bf16[1,3584,512]{2,1,0:T(8,128)(2,1)S(1)} %copy-done.2), kind=kOutput, calls=%fused_computation.16 | convolution fusion | flops 1879310336 | bytes 7864320 | tf_op jit(solution)/shard_map/lrh,lhf->lrf/dot_general | solution.py:63
  121.6 29.0 %all-reduce.3.cloned.1.call-done = (bf16[1,512,512]{2,1,0:T(8,128)(2,1)}, bf16[1,512,512]{2,1,0:T(8,128)(2,1)}) async-done(((bf16[1,512,512]{2,1,0:T(8,128)(2,1)}, bf16[1,512,512]{2,1,0:T(8,128)(2,1)}), (bf16[1,512,512]{2,1,0:T(8,128)(2,1)}, bf16[1,512,512]{2,1,0:T(8,128)(2,1)})) %all-reduce.3.cloned.1.call-update) | async-done | bytes 1048592 | tf_op jit(solution)/shard_map/psum | solution.py:67
  150.6 6.4 %fusion.1 = bf16[1,512,3584]{2,1,0:T(8,128)(2,1)} fusion(bf16[1,512,3584]{2,1,0:T(8,128)(2,1)} %param.11, bf16[1,512,512]{2,1,0:T(8,128)(2,1)} %get-tuple-element.5, bf16[1,512,512]{2,1,0:T(8,128)(2,1)} %get-tuple-element.6), kind=kOutput, calls=%fused_computation.3 | convolution fusion | flops 1882980352 | bytes 8388608 | tf_op jit(solution)/shard_map/lrf,lfh->lrh/dot_general | solution.py:70
  157.0 16.5 %copy.38 = bf16[1,512,3584]{1,0,2:T(2,128)(2,1)} copy(bf16[1,512,3584]{2,1,0:T(8,128)(2,1)} %fusion.1) | data formatting | bytes 7340032
  173.5 6.1 %copy.51 = bf16[3584,1,512]{2,0,1:T(8,128)(2,1)} copy(bf16[3584,1,512]{2,1,0:T(2,128)(2,1)} %bitcast.69) | data formatting | bytes 7340032
  179.6 45.8 %reduce-scatter.4.cloned.1.call-done = bf16[896,512]{1,0:T(8,128)(2,1)} async-done(((bf16[3584,512]{1,0:T(8,128)(2,1)}), bf16[896,512]{1,0:T(8,128)(2,1)}) %reduce-scatter.4.cloned.1.call-update) | async-done | bytes 917520
  225.5 2.1 reshape_bitcast_fusion
  227.6 1.3 copy.39
  228.9 1.0 copy.30
  229.9 9.6 %all-to-all-start.2 = ((bf16[1,2,32,8,896]{4,3,1,0,2:T(8,128)(2,1)}), bf16[1,2,32,8,896]{4,3,1,0,2:T(8,128)(2,1)S(1)}, u32[]{:S(2)}, u32[]{:S(2)}) async-start(bf16[1,2,32,8,896]{4,3,1,0,2:T(8,128)(2,1)} %copy.30), calls=%async_computation.2 | async-start | bytes 1835008 | tf_op jit(solution)/shard_map/all_to_all | solution.py:12
  239.8 23.1 %all-to-all-done.2 = bf16[1,2,32,8,896]{4,3,1,0,2:T(8,128)(2,1)S(1)} async-done(((bf16[1,2,32,8,896]{4,3,1,0,2:T(8,128)(2,1)}), bf16[1,2,32,8,896]{4,3,1,0,2:T(8,128)(2,1)S(1)}, u32[]{:S(2)}, u32[]{:S(2)}) %all-to-all-start.2) | async-done | bytes 917536 | tf_op jit(solution)/shard_map/all_to_all | solution.py:12
  263.1 7.2 %all_to_all.22 = bf16[1,2,32,8,896]{4,2,3,0,1:T(8,128)(2,1)S(1)} all-to-all(bf16[1,2,32,8,896]{4,2,3,0,1:T(8,128)(2,1)S(1)} %copy.31), channel_id=1, replica_groups=mesh['expert'=32,'tensor'=4,'dp'=2] {'dp'}, dimensions={1} | all-to-all | bytes 1835008 | tf_op jit(solution)/shard_map/all_to_all | solution.py:80
  270.3 0.4 fusion.19
  270.8 0.7 copy.33
  (20 shorter events, 1.3 us)
Async XLA Ops:
  6.5 144.1 %all-reduce.3.cloned.1.call-start = ((), (), s32[]{:S(2)}) async-start(), calls=%async_computation.6 | async-start | bytes 2097152 | tf_op jit(solution)/shard_map/psum | solution.py:67
  113.7 2.0 copy-start.1
  115.8 2.9 %copy-start.2 = (bf16[1,3584,512]{2,1,0:T(8,128)(2,1)S(1)}, bf16[1,3584,512]{2,1,0:T(8,128)(2,1)}, u32[]{:S(2)}) copy-start(bf16[1,3584,512]{2,1,0:T(8,128)(2,1)} %param.9) | copy-start | bytes 11010052
  121.6 103.9 %reduce-scatter.4.cloned.1.call-start = ((), (), s32[]{:S(2)}) async-start(), calls=%async_computation.5 | async-start | bytes 4587520
  227.6 11.9 %copy-start = (f32[16,8]{0,1:T(8,128)S(1)}, f32[16,8]{0,1:T(8,128)}, u32[]{:S(2)}) copy-start(f32[16,8]{0,1:T(8,128)} %param.8) | copy-start | bytes 1540
  229.9 33.1 %all-to-all-start.2 = ((bf16[1,2,32,8,896]{4,3,1,0,2:T(8,128)(2,1)}), bf16[1,2,32,8,896]{4,3,1,0,2:T(8,128)(2,1)S(1)}, u32[]{:S(2)}, u32[]{:S(2)}) async-start(bf16[1,2,32,8,896]{4,3,1,0,2:T(8,128)(2,1)} %copy.30), calls=%async_computation.2 | async-start | bytes 1835008 | tf_op jit(solution)/shard_map/all_to_all | solution.py:12
Sparse Core Ops, SparseCore 0:
  121.7 28.8 all-reduce.2
  179.7 45.6 reduce-scatter.3
where the time goes:
time: 279 us; the launch traced here: 278 us
  blocking collectives  110 us (39%)
  waiting for transfers between devices  98 us (35%)
  local copies, waits for them, and re-layouts  31.8 us (11%)
  matrix products  15.1 us (5%)
  between operations  13.5 us (5%)
  starting transfers between devices  9.6 us (3%)
    all_to_all x1, blocking collectives, route_over_experts(): lax.all_to_all(blocks, 'expert', split_axis=2, concat_axis=2, tiled=True)  93.1 us
    unnamed x3, waiting for transfers between devices  45.9 us
    psum x1, waiting for transfers between devices, on_device(): lax.psum(up.astype(jnp.bfloat16), 'dp').astype(jnp.float32)  29 us
    unnamed x11, local copies, waits for them, and re-layouts  28.5 us
    all_to_all x1, waiting for transfers between devices, route_over_experts(): lax.all_to_all(blocks, 'expert', split_axis=2, concat_axis=2, tiled=True)  23.1 us
    all_to_all x1, starting transfers between devices, route_over_experts(): lax.all_to_all(blocks, 'expert', split_axis=2, concat_axis=2, tiled=True)  9.56 us
    all_to_all x1, blocking collectives, on_device(): lax.all_to_all(outgoing, 'dp', split_axis=1, concat_axis=1, tiled=True)  9.55 us
    all_to_all x1, blocking collectives, on_device(): lax.all_to_all(returned, 'dp', split_axis=1, concat_axis=1, tiled=True)  7.17 us
  transfers between devices with their start and end apart: 3, of which 3 were waited for; matrix products, arithmetic and copies ran while one was open for 0% of the time, Pallas kernels for 0%

commit v1 on v0

--- a/solution.py
+++ b/solution.py
@@ -64,7 +64,9 @@
     up = jnp.einsum("lrh,lhf->lrf", arrived, up_weight, preferred_element_type=jnp.float32)
     gate, up = (
         lax.psum(gate.astype(jnp.bfloat16), "dp").astype(jnp.float32),
-        lax.psum(up.astype(jnp.bfloat16), "dp").astype(jnp.float32),
+        jnp.sum(jax.lax.all_gather(up.astype(jnp.bfloat16), axis_name="dp"), axis=0).astype(
+            jnp.float32
+        ),
     )
     hidden = (jax.nn.silu(gate) * up).astype(jnp.bfloat16)
     partial_value = jnp.einsum(

time: 279 us -> 295 us (1.057)
  waiting for transfers between devices: 98 us -> 108 us
  matrix products: 15.1 us -> 18.1 us
    all_gather x0 -> x1, waiting for transfers between devices: none -> 6.84 us  [on_device(): jax.lax.all_gather(up.astype(jnp.bfloat16), axis_name='dp')]
    dot_general x1, matrix products: 2.89 us -> 6.02 us  [on_device(): jnp.einsum('lrh,lhf->lrf', arrived, gate_weight, preferred_element_type=j...]
    unnamed x3 -> x4, waiting for transfers between devices: 45.9 us -> 45.9 us
  transfers between devices with their start and end apart: 3 -> 4, of which waited for: 3 -> 4; matrix products, arithmetic and copies ran while one was open for 0% -> 3% of each run, Pallas kernels for 0% -> 0%
where the time goes in v1:
time: 295 us; the launch traced here: 294 us
  blocking collectives  110 us (37%)
  waiting for transfers between devices  108 us (37%)
  local copies, waits for them, and re-layouts  33.1 us (11%)
  matrix products  18.1 us (6%)
  between operations  13.2 us (4%)
  starting transfers between devices  9.65 us (3%)
    all_to_all x1, blocking collectives, route_over_experts(): lax.all_to_all(blocks, 'expert', split_axis=2, concat_axis=2, tiled=True)  93.1 us
    unnamed x4, waiting for transfers between devices  45.9 us
    psum x1, waiting for transfers between devices, on_device(): lax.psum(gate.astype(jnp.bfloat16), 'dp').astype(jnp.float32)  31.8 us
    unnamed x11, local copies, waits for them, and re-layouts  29.8 us
    all_to_all x1, waiting for transfers between devices, route_over_experts(): lax.all_to_all(blocks, 'expert', split_axis=2, concat_axis=2, tiled=True)  23.1 us
    all_to_all x1, starting transfers between devices, route_over_experts(): lax.all_to_all(blocks, 'expert', split_axis=2, concat_axis=2, tiled=True)  9.56 us
    all_to_all x1, blocking collectives, on_device(): lax.all_to_all(outgoing, 'dp', split_axis=1, concat_axis=1, tiled=True)  9.55 us
    all_to_all x1, blocking collectives, on_device(): lax.all_to_all(returned, 'dp', split_axis=1, concat_axis=1, tiled=True)  7.17 us
  transfers between devices with their start and end apart: 4, of which 4 were waited for; matrix products, arithmetic and copies ran while one was open for 3% of the time, Pallas kernels for 0%

profile of v1, /device:TPU:1, one launch (start us, length us, event | category | flops | bytes accessed | tf_op | source)
XLA Modules:
  0.0 293.6 jit_solution(17217202902236917258)
XLA Ops:
  6.5 0.8 copy.22
  8.3 2.0 fusion
  10.6 9.5 %all_to_all.20 = bf16[1,2,32,8,3584]{4,3,2,0,1:T(8,128)(2,1)S(1)} all-to-all(bf16[1,2,32,8,3584]{4,3,2,0,1:T(8,128)(2,1)S(1)} %copy.27), channel_id=1, replica_groups=mesh['expert'=32,'tensor'=4,'dp'=2] {'dp'}, dimensions={1} | all-to-all | bytes 7340032 | tf_op jit(solution)/shard_map/all_to_all | solution.py:59
  20.1 0.5 copy.28
  20.6 93.1 %all_to_all.21 = bf16[1,2,32,8,3584]{4,3,1,0,2:T(8,128)(2,1)S(1)} all-to-all(bf16[1,2,32,8,3584]{4,3,1,0,2:T(8,128)(2,1)S(1)} %copy.28), channel_id=1, replica_groups=mesh['expert'=32,'tensor'=4,'dp'=2] {'expert'}, dimensions={2} | all-to-all | bytes 7340032 | tf_op jit(solution)/shard_map/all_to_all | solution.py:12
  114.0 1.9 copy-done
  115.9 1.2 copy-done.2
  117.1 2.9 fusion.10
  120.0 6.0 %fusion.13 = bf16[1,512,512]{2,1,0:T(8,128)(2,1)} fusion(bf16[512,3584]{1,0:T(8,128)(2,1)} %bitcast.75, bf16[1,3584,512]{2,1,0:T(8,128)(2,1)} %param.9), kind=kOutput, calls=%fused_computation.15 | convolution fusion | flops 1879310336 | bytes 7864320 | tf_op jit(solution)/shard_map/lrh,lhf->lrf/dot_general | solution.py:63
  126.1 6.8 %all-gather.3.cloned.1.call-done = bf16[1024,512]{1,0:T(8,128)(2,1)} async-done(((bf16[512,512]{1,0:T(8,128)(2,1)}), bf16[1024,512]{1,0:T(8,128)(2,1)}) %all-gather.3.cloned.1.call-update) | async-done | bytes 1048592 | tf_op jit(solution)/shard_map/all_gather | solution.py:67
  133.0 1.7 reduce.2
  134.6 31.8 %all-reduce.2.cloned.1.call-done = bf16[1,512,512]{2,1,0:T(8,128)(2,1)} async-done(((bf16[1,512,512]{2,1,0:T(8,128)(2,1)}), bf16[1,512,512]{2,1,0:T(8,128)(2,1)}) %all-reduce.2.cloned.1.call-update) | async-done | bytes 524304 | tf_op jit(solution)/shard_map/psum | solution.py:66
  166.4 6.2 %fusion.1 = bf16[1,512,3584]{2,1,0:T(8,128)(2,1)} fusion(bf16[1,512,3584]{2,1,0:T(8,128)(2,1)} %param.11, bf16[1,512,512]{2,1,0:T(8,128)(2,1)} %all-reduce.2.cloned.1.call-done, bf16[512,512]{1,0:T(8,128)(2,1)S(1)} %reduce.2), kind=kOutput, calls=%fused_computation.3 | convolution fusion | flops 1882980352 | bytes 8388608 | tf_op jit(solution)/shard_map/lrf,lfh->lrh/dot_general | solution.py:72
  172.6 16.5 %copy.38 = bf16[1,512,3584]{1,0,2:T(2,128)(2,1)} copy(bf16[1,512,3584]{2,1,0:T(8,128)(2,1)} %fusion.1) | data formatting | bytes 7340032
  189.1 6.1 %copy.51 = bf16[3584,1,512]{2,0,1:T(8,128)(2,1)} copy(bf16[3584,1,512]{2,1,0:T(2,128)(2,1)} %bitcast.72) | data formatting | bytes 7340032
  195.2 45.8 %reduce-scatter.4.cloned.1.call-done = bf16[896,512]{1,0:T(8,128)(2,1)} async-done(((bf16[3584,512]{1,0:T(8,128)(2,1)}), bf16[896,512]{1,0:T(8,128)(2,1)}) %reduce-scatter.4.cloned.1.call-update) | async-done | bytes 917520
  241.1 2.1 reshape_bitcast_fusion
  243.2 1.3 copy.39
  244.5 1.0 copy.30
  245.5 9.6 %all-to-all-start.2 = ((bf16[1,2,32,8,896]{4,3,1,0,2:T(8,128)(2,1)}), bf16[1,2,32,8,896]{4,3,1,0,2:T(8,128)(2,1)S(1)}, u32[]{:S(2)}, u32[]{:S(2)}) async-start(bf16[1,2,32,8,896]{4,3,1,0,2:T(8,128)(2,1)} %copy.30), calls=%async_computation.2 | async-start | bytes 1835008 | tf_op jit(solution)/shard_map/all_to_all | solution.py:12
  255.4 23.1 %all-to-all-done.2 = bf16[1,2,32,8,896]{4,3,1,0,2:T(8,128)(2,1)S(1)} async-done(((bf16[1,2,32,8,896]{4,3,1,0,2:T(8,128)(2,1)}), bf16[1,2,32,8,896]{4,3,1,0,2:T(8,128)(2,1)S(1)}, u32[]{:S(2)}, u32[]{:S(2)}) %all-to-all-start.2) | async-done | bytes 917536 | tf_op jit(solution)/shard_map/all_to_all | solution.py:12
  278.8 7.2 %all_to_all.22 = bf16[1,2,32,8,896]{4,2,3,0,1:T(8,128)(2,1)S(1)} all-to-all(bf16[1,2,32,8,896]{4,2,3,0,1:T(8,128)(2,1)S(1)} %copy.31), channel_id=1, replica_groups=mesh['expert'=32,'tensor'=4,'dp'=2] {'dp'}, dimensions={1} | all-to-all | bytes 1835008 | tf_op jit(solution)/shard_map/all_to_all | solution.py:82
  285.9 0.4 fusion.16
  286.4 0.7 copy.33
  (24 shorter events, 2.1 us)
Async XLA Ops:
  6.5 126.4 %all-gather.3.cloned.1.call-start = ((), (), s32[]{:S(2)}) async-start(), calls=%async_computation.6 | async-start | bytes 1572864 | tf_op jit(solution)/shard_map/all_gather | solution.py:67
  113.7 3.4 %copy-start.2 = (bf16[1,3584,512]{2,1,0:T(8,128)(2,1)S(1)}, bf16[1,3584,512]{2,1,0:T(8,128)(2,1)}, u32[]{:S(2)}) copy-start(bf16[1,3584,512]{2,1,0:T(8,128)(2,1)} %param.10) | copy-start | bytes 11010052
  114.0 1.9 copy-start
  120.0 46.4 %all-reduce.2.cloned.1.call-start = ((), (), s32[]{:S(2)}) async-start(), calls=%async_computation.5 | async-start | bytes 1048576 | tf_op jit(solution)/shard_map/psum | solution.py:66
  126.1 115.0 %reduce-scatter.4.cloned.1.call-start = ((), (), s32[]{:S(2)}) async-start(), calls=%async_computation.7 | async-start | bytes 4587520
  243.2 11.9 %copy-start.1 = (f32[16,8]{0,1:T(8,128)S(1)}, f32[16,8]{0,1:T(8,128)}, u32[]{:S(2)}) copy-start(f32[16,8]{0,1:T(8,128)} %param.8) | copy-start | bytes 1540
  245.5 33.1 %all-to-all-start.2 = ((bf16[1,2,32,8,896]{4,3,1,0,2:T(8,128)(2,1)}), bf16[1,2,32,8,896]{4,3,1,0,2:T(8,128)(2,1)S(1)}, u32[]{:S(2)}, u32[]{:S(2)}) async-start(bf16[1,2,32,8,896]{4,3,1,0,2:T(8,128)(2,1)} %copy.30), calls=%async_computation.2 | async-start | bytes 1835008 | tf_op jit(solution)/shard_map/all_to_all | solution.py:12
Sparse Core Ops, SparseCore 0:
  120.1 12.8 all-gather.2
  135.5 30.7 all-reduce.1
  195.4 45.6 reduce-scatter.3
